TPU v7x, 128 devices: a whole 4x4x4 slice. The times are simulated.
128 devices in a mesh: row: 8 (over z, core), col: 16 (over y, x).
Axes of the slice: x: 4, y: 4, z: 4, core: 2. Of those that a mesh axis runs over, the one named last changes fastest.
Arguments:
- amp_tiles: float32 [16, 32, 256, 256], P('row', 'col'), may hold values from -6 to 6
- int_tiles: float32 [32, 32, 256, 256], P('col', 'row'), may hold values from -0.125 to 0.125
- resid_init: float32 [16, 32, 256, 256], P('row', 'col'), may hold values from -6 to 6
- triples: int32 [8, 16, 3, 32], P('row', 'col'), may hold values from 0 to 1023, as said below
Outputs:
- resid_out: float32 [16, 32, 256, 256], P('row', 'col')
Inputs may be any that keep to these rules, and one draw needn't show every extreme that they name: Each triple names tiles (i, j), (j, k), (i, k) with one i, j, k. The amplitude tile of every triple on device (r, c) is one that device holds. For every device and every column index q, exactly 2 distinct residual tiles held at (r, q) are named by that device's triples, each by exactly one of that device's triples. No triple is listed twice; the order of triples on a device is arbitrary.
All inputs are finite; a program needn't handle non-finite values.
Results may differ from a plain program's by a relative error of at most 0.0001.
Values sent between devices are 32-bit elements; how exact they have to be, the bound alone decides.
No kernel may reach another device: no remote copies, remote signals or barrier semaphores. Data moves between devices by JAX's collectives and lax.ppermute only.
A program may use at most 128 MiB of HBM per device.

v0:
```python
import jax
import jax.numpy as jnp
from jax import lax
from jax.sharding import PartitionSpec as P


def on_device(amp_tiles, int_tiles, resid_init, triples):
    occ_blocks = amp_tiles.shape[0]
    vir_blocks = amp_tiles.shape[1]
    width = amp_tiles.shape[2]
    own_k = resid_init.shape[1]
    col_count = lax.axis_size("col")
    all_k = own_k * col_count
    all_j = vir_blocks * col_count
    row_place = lax.axis_index("row")
    col_place = lax.axis_index("col")
    listing = triples[0, 0]
    amp_ids = listing[0]
    int_ids = listing[1]
    res_ids = listing[2]
    amp_occ = amp_ids // all_j - row_place * occ_blocks
    amp_vir = amp_ids % all_j - col_place * vir_blocks
    int_vir = int_ids // all_k - col_place * vir_blocks
    int_col = int_ids % all_k
    res_occ = res_ids // all_k - row_place * occ_blocks
    res_col = res_ids % all_k
    amp_index = amp_occ * vir_blocks + amp_vir
    int_index = int_vir * all_k + int_col
    gathered = lax.all_gather(int_tiles, "row", axis=1, tiled=True)
    amp_flat = amp_tiles.reshape(-1, width, width)
    int_flat = gathered.reshape(-1, width, width)
    target = res_occ * all_k + res_col
    slots_total = occ_blocks * all_k
    block = 8

    def add_block(partial_value, pieces):
        amp_pick, int_pick, target_pick = pieces
        products = jnp.einsum(
            "bxy,byz->bxz",
            amp_flat[amp_pick],
            int_flat[int_pick],
            precision=lax.Precision.HIGHEST,
            preferred_element_type=jnp.float32,
        )
        return (partial_value.at[target_pick].add(products), None)

    start = jnp.zeros((slots_total, width, width), jnp.float32)
    pieces = (amp_index.reshape(-1, block), int_index.reshape(-1, block), target.reshape(-1, block))
    partial_value, _ = lax.scan(add_block, start, pieces)
    summed = lax.psum_scatter(
        partial_value.reshape(occ_blocks, all_k, width, width),
        "col",
        scatter_dimension=1,
        tiled=True,
    )
    return resid_init + summed


def solution(mesh):
    return jax.shard_map(
        on_device,
        mesh=mesh,
        in_specs=(
            P("row", "col", None, None),
            P("col", "row", None, None),
            P("row", "col", None, None),
            P("row", "col", None, None),
        ),
        out_specs=P("row", "col", None, None),
        check_vma=False,
    )
```

profile of v0, /device:TPU:1, one launch (start us, length us, event | category | flops | bytes accessed | tf_op | source)
XLA Modules:
  0.0 409.5 jit_solution(13803242583573978467)
XLA Ops:
  6.5 0.0 copy-start.2
  6.5 0.0 all-gather.2.cloned.1.call-start
  6.5 0.7 all-gather.2.cloned.1.call-update
  7.3 0.0 all-reduce.3.cloned.1.call-start
  7.3 0.0 copy-done.2
  7.3 0.1 squeeze.20
  7.4 0.1 squeeze.21
  7.5 0.1 squeeze.22
  7.6 90.2 %all-gather.2.cloned.1.call-done = f32[2,32,256,256]{3,2,1,0:T(8,128)} async-done(((f32[2,4,256,256]{3,2,1,0:T(8,128)}), f32[2,32,256,256]{3,2,1,0:T(8,128)}) %all-gather.2.cloned.1.call-update) | async-done | bytes 16777232 | tf_op jit(solution)/shard_map/all_gather | solution.py:29
  97.9 0.0 copy-start
  97.9 7.8 %broadcast_in_dim.2 = f32[64,256,256]{2,1,0:T(8,128)} broadcast(f32[]{:T(128)} %constant.72.clone.1), dimensions={} | broadcast | bytes 16777220 | tf_op jit(solution)/shard_map/broadcast_in_dim | solution.py:47
  105.6 0.0 copy-done
  105.6 74.2 %while.10 = (s32[]{:T(128)}, f32[64,256,256]{2,1,0:T(8,128)}, s32[4,8]{1,0:T(4,128)S(1)}, s32[4,8]{1,0:T(4,128)S(1)}, f32[4,256,256]{2,1,0:T(8,128)S(1)}, /*inde...) while((s32[]{:T(128)}, f32[64,256,256]{2,1,0:T(8,128)}, s32[4,8]{1,0:T(4,128)S(1)}, ...), condition=%wide.region_2.3_spmd, body=%wide.region_0.2_spmd.sunk | while | flops 1611139200 | bytes 20980156 | solution.py:49
  105.7 2.0 gather_fusion
  107.7 7.8 %gather_fusion.1 = f32[8,256,256]{2,1,0:T(8,128)} fusion(f32[64,256,256]{2,1,0:T(8,128)} %get-tuple-element.133, s32[1024]{0:T(1024)S(1)} %pad_clamp_fusion.5), kind=kCustom, calls=%fused_computation.1.clone.1 | custom fusion | bytes 4194336 | tf_op jit(solution)/shard_map/while/body/eval_jaxpr/gather | solution.py:41
  115.5 4.3 %fusion.34 = f32[8,256,256]{2,1,0:T(8,128)S(1)} fusion(f32[8,256,256]{2,1,0:T(8,128)} %gather_fusion, f32[8,256,256]{2,1,0:T(8,128)} %gather_fusion.1), kind=kOutput, calls=%fused_computation.55.clone.1 | convolution fusion | flops 1610612736 | bytes 6291456 | tf_op jit(solution)/shard_map/while/body/eval_jaxpr/bxy,byz->bxz/dot_general | solution.py:38
  119.8 4.4 %scatter_fusion = f32[64,256,256]{2,1,0:T(8,128)} fusion(f32[64,256,256]{2,1,0:T(8,128)} %get-tuple-element.120, s32[8]{0:T(128)S(1)} %get-tuple-element.109, f32[8,256,256]{2,1,0:T(8,128)S(1)} %fusion.34), kind=kCustom, calls=%fused_computation.2.clone.1 | custom fusion | flops 524288 | bytes 6291488 | tf_op jit(solution)/shard_map/while/body/eval_jaxpr/scatter-add | solution.py:45
  124.2 2.0 gather_fusion
  126.2 7.8 %gather_fusion.1 = f32[8,256,256]{2,1,0:T(8,128)} fusion(f32[64,256,256]{2,1,0:T(8,128)} %get-tuple-element.133, s32[1024]{0:T(1024)S(1)} %pad_clamp_fusion.5), kind=kCustom, calls=%fused_computation.1.clone.1 | custom fusion | bytes 4194336 | tf_op jit(solution)/shard_map/while/body/eval_jaxpr/gather | solution.py:41
  134.0 4.3 %fusion.34 = f32[8,256,256]{2,1,0:T(8,128)S(1)} fusion(f32[8,256,256]{2,1,0:T(8,128)} %gather_fusion, f32[8,256,256]{2,1,0:T(8,128)} %gather_fusion.1), kind=kOutput, calls=%fused_computation.55.clone.1 | convolution fusion | flops 1610612736 | bytes 6291456 | tf_op jit(solution)/shard_map/while/body/eval_jaxpr/bxy,byz->bxz/dot_general | solution.py:38
  138.3 4.4 %scatter_fusion = f32[64,256,256]{2,1,0:T(8,128)} fusion(f32[64,256,256]{2,1,0:T(8,128)} %get-tuple-element.120, s32[8]{0:T(128)S(1)} %get-tuple-element.109, f32[8,256,256]{2,1,0:T(8,128)S(1)} %fusion.34), kind=kCustom, calls=%fused_computation.2.clone.1 | custom fusion | flops 524288 | bytes 6291488 | tf_op jit(solution)/shard_map/while/body/eval_jaxpr/scatter-add | solution.py:45
  142.8 2.0 gather_fusion
  144.8 7.8 %gather_fusion.1 = f32[8,256,256]{2,1,0:T(8,128)} fusion(f32[64,256,256]{2,1,0:T(8,128)} %get-tuple-element.133, s32[1024]{0:T(1024)S(1)} %pad_clamp_fusion.5), kind=kCustom, calls=%fused_computation.1.clone.1 | custom fusion | bytes 4194336 | tf_op jit(solution)/shard_map/while/body/eval_jaxpr/gather | solution.py:41
  152.6 4.3 %fusion.34 = f32[8,256,256]{2,1,0:T(8,128)S(1)} fusion(f32[8,256,256]{2,1,0:T(8,128)} %gather_fusion, f32[8,256,256]{2,1,0:T(8,128)} %gather_fusion.1), kind=kOutput, calls=%fused_computation.55.clone.1 | convolution fusion | flops 1610612736 | bytes 6291456 | tf_op jit(solution)/shard_map/while/body/eval_jaxpr/bxy,byz->bxz/dot_general | solution.py:38
  156.9 4.4 %scatter_fusion = f32[64,256,256]{2,1,0:T(8,128)} fusion(f32[64,256,256]{2,1,0:T(8,128)} %get-tuple-element.120, s32[8]{0:T(128)S(1)} %get-tuple-element.109, f32[8,256,256]{2,1,0:T(8,128)S(1)} %fusion.34), kind=kCustom, calls=%fused_computation.2.clone.1 | custom fusion | flops 524288 | bytes 6291488 | tf_op jit(solution)/shard_map/while/body/eval_jaxpr/scatter-add | solution.py:45
  161.3 2.0 gather_fusion
  163.3 7.8 %gather_fusion.1 = f32[8,256,256]{2,1,0:T(8,128)} fusion(f32[64,256,256]{2,1,0:T(8,128)} %get-tuple-element.133, s32[1024]{0:T(1024)S(1)} %pad_clamp_fusion.5), kind=kCustom, calls=%fused_computation.1.clone.1 | custom fusion | bytes 4194336 | tf_op jit(solution)/shard_map/while/body/eval_jaxpr/gather | solution.py:41
  171.2 4.3 %fusion.34 = f32[8,256,256]{2,1,0:T(8,128)S(1)} fusion(f32[8,256,256]{2,1,0:T(8,128)} %gather_fusion, f32[8,256,256]{2,1,0:T(8,128)} %gather_fusion.1), kind=kOutput, calls=%fused_computation.55.clone.1 | convolution fusion | flops 1610612736 | bytes 6291456 | tf_op jit(solution)/shard_map/while/body/eval_jaxpr/bxy,byz->bxz/dot_general | solution.py:38
  175.5 4.4 %scatter_fusion = f32[64,256,256]{2,1,0:T(8,128)} fusion(f32[64,256,256]{2,1,0:T(8,128)} %get-tuple-element.120, s32[8]{0:T(128)S(1)} %get-tuple-element.109, f32[8,256,256]{2,1,0:T(8,128)S(1)} %fusion.34), kind=kCustom, calls=%fused_computation.2.clone.1 | custom fusion | flops 524288 | bytes 6291488 | tf_op jit(solution)/shard_map/while/body/eval_jaxpr/scatter-add | solution.py:45
  179.8 0.0 copy-start.3
  179.8 0.0 copy-start.1
  179.8 0.0 all-reduce.3.cloned.1.call-update
  179.9 0.6 copy-done.3
  180.5 0.6 dynamic-slice
  181.7 218.7 %all-reduce.3.cloned.1.call-done = f32[2,32,256,256]{3,2,1,0:T(8,128)} async-done(((f32[2,32,256,256]{3,2,1,0:T(8,128)}), f32[2,32,256,256]{3,2,1,0:T(8,128)}) %all-reduce.3.cloned.1.call-update) | async-done | bytes 16777232
  400.4 0.0 copy-done.1
  400.4 2.3 dynamic-slice_add_fusion
  (19 shorter events, 0.2 us)
Async XLA Ops:
  6.5 0.8 copy-start.2
  6.5 91.3 %all-gather.2.cloned.1.call-start = ((), (), s32[]{:S(2)}) async-start(), calls=%async_computation | async-start | bytes 18874368 | tf_op jit(solution)/shard_map/all_gather | solution.py:29
  7.3 393.1 %all-reduce.3.cloned.1.call-start = ((), (), s32[]{:S(2)}) async-start(), calls=%async_computation.1 | async-start | bytes 33554432
  97.9 7.8 %copy-start = (f32[2,2,256,256]{3,2,1,0:T(8,128)S(1)}, f32[2,2,256,256]{3,2,1,0:T(8,128)}, u32[]{:S(2)}) copy-start(f32[2,2,256,256]{3,2,1,0:T(8,128)} %param.6) | copy-start | bytes 3145732
  179.8 0.7 copy-start.3
  179.8 220.5 %copy-start.1 = (f32[2,2,256,256]{3,2,1,0:T(8,128)S(1)}, f32[2,2,256,256]{3,2,1,0:T(8,128)}, u32[]{:S(2)}) copy-start(f32[2,2,256,256]{3,2,1,0:T(8,128)} %param.8) | copy-start | bytes 3145732
Sparse Core Ops, SparseCore 0:
  9.1 88.7 all-gather.1
  180.0 220.3 all-reduce.2
where the time goes:
time: 410 us
  waiting for transfers between devices  310 us (76%)
  local copies, waits for them, and re-layouts  48.5 us (12%)
  other arithmetic  20 us (5%)
  matrix products  17.2 us (4%)
  between operations  14.1 us (3%)
    unnamed x3, waiting for transfers between devices  219 us
    all_gather x1, waiting for transfers between devices, on_device(): gathered = lax.all_gather(int_tiles, 'row', axis=1, tiled=True)  90.2 us
    gather x4, local copies, waits for them, and re-layouts, add_block(): int_flat[int_pick]  31.3 us
    scatter-add x4, other arithmetic, add_block(): return (partial_value.at[target_pick].add(products), None)  17.5 us
    dot_general x4, matrix products, add_block(): jnp.einsum('bxy,byz->bxz', amp_flat[amp_pick], int_flat[int_pick], precis...  17.2 us
  transfers between devices with their start and end apart: 2, of which 2 were waited for; matrix products, arithmetic and copies ran while one was open for 0% of the time, Pallas kernels for 0%

commit v1 on v0

--- a/solution.py
+++ b/solution.py
@@ -2,6 +2,19 @@
 import jax.numpy as jnp
 from jax import lax
 from jax.sharding import PartitionSpec as P
+
+
+def ring_gather(x, axis, dim):
+    ways = lax.axis_size(axis)
+    up = [(d, (d + 1) % ways) for d in range(ways)]
+    down = [(d, (d - 1) % ways) for d in range(ways)]
+    earlier, later = ([x], [x])
+    for _ in range(ways // 2):
+        earlier.append(lax.ppermute(earlier[-1], axis, up))
+    for _ in range((ways - 1) // 2):
+        later.append(lax.ppermute(later[-1], axis, down))
+    line = jnp.concatenate([*earlier[::-1], *later[1:]], axis=dim)
+    return jnp.roll(line, (lax.axis_index(axis) - ways // 2) * x.shape[dim], axis=dim)
 
 
 def on_device(amp_tiles, int_tiles, resid_init, triples):
@@ -26,7 +39,7 @@
     res_col = res_ids % all_k
     amp_index = amp_occ * vir_blocks + amp_vir
     int_index = int_vir * all_k + int_col
-    gathered = lax.all_gather(int_tiles, "row", axis=1, tiled=True)
+    gathered = ring_gather(int_tiles, "row", 1)
     amp_flat = amp_tiles.reshape(-1, width, width)
     int_flat = gathered.reshape(-1, width, width)
     target = res_occ * all_k + res_col

time: 410 us -> 454 us (1.11)
  local copies, waits for them, and re-layouts: 48.5 us -> 77.8 us
  starting transfers between devices: 0.04 us -> 13.8 us
    all_gather x1 -> x0, waiting for transfers between devices: 90.2 us -> none  [on_device(): gathered = lax.all_gather(int_tiles, 'row', axis=1, tiled=True)]
    ppermute x0 -> x7, waiting for transfers between devices: none -> 86.8 us  [the longest x4 84.2 us: ring_gather(): earlier.append(lax.ppermute(earlier[-1], axis, up))]
    unnamed x9 -> x36, local copies, waits for them, and re-layouts: 1.22 us -> 21.5 us
    ppermute x0 -> x7, starting transfers between devices: none -> 13.8 us  [the longest x4 10.5 us: ring_gather(): earlier.append(lax.ppermute(earlier[-1], axis, up))]
    dynamic_slice x0 -> x1, local copies, waits for them, and re-layouts: none -> 6.35 us  [ring_gather(): jnp.roll(line, (lax.axis_index(axis) - ways // 2) * x.shape[dim], axis=dim)]
    unnamed x3 -> x2, waiting for transfers between devices: 219 us -> 223 us
  transfers between devices with their start and end apart: 2 -> 8, of which waited for: 2 -> 7; matrix products, arithmetic and copies ran while one was open for 0% -> 2% of each run, Pallas kernels for 0% -> 0%
where the time goes in v1:
time: 454 us; the launch traced here: 453 us
  waiting for transfers between devices  310 us (68%)
  local copies, waits for them, and re-layouts  77.8 us (17%)
  other arithmetic  20 us (4%)
  matrix products  17.2 us (4%)
  between operations  14.3 us (3%)
  starting transfers between devices  13.8 us (3%)
    unnamed x2, waiting for transfers between devices  223 us
    ppermute x4, waiting for transfers between devices, ring_gather(): earlier.append(lax.ppermute(earlier[-1], axis, up))  84.2 us
    gather x4, local copies, waits for them, and re-layouts, add_block(): int_flat[int_pick]  31.3 us
    unnamed x36, local copies, waits for them, and re-layouts  21.5 us
    scatter-add x4, other arithmetic, add_block(): return (partial_value.at[target_pick].add(products), None)  17.5 us
    dot_general x4, matrix products, add_block(): jnp.einsum('bxy,byz->bxz', amp_flat[amp_pick], int_flat[int_pick], precis...  17.2 us
    ppermute x4, starting transfers between devices, ring_gather(): earlier.append(lax.ppermute(earlier[-1], axis, up))  10.5 us
  transfers between devices with their start and end apart: 8, of which 7 were waited for; matrix products, arithmetic and copies ran while one was open for 2% of the time, Pallas kernels for 0%

profile of v1, /device:TPU:1, one launch (start us, length us, event | category | flops | bytes accessed | tf_op | source)
XLA Modules:
  0.0 453.2 jit_solution(12098027820226899846)
XLA Ops:
  6.5 3.0 collective-permute-start
  9.6 23.3 %collective-permute-done = f32[2,4,256,256]{3,2,1,0:T(8,128)S(1)} collective-permute-done((f32[2,4,256,256]{3,2,1,0:T(8,128)}, f32[2,4,256,256]{3,2,1,0:T(8,128)S(1)}, u32[]{:S(2)}, u32[]{:S(2)}) %collective-permute-start) | collective-permute-done | bytes 2097184 | tf_op jit(solution)/shard_map/ppermute | solution.py:13
  32.9 1.3 copy-done.2
  34.2 2.4 collective-permute-start.1
  36.9 22.7 %collective-permute-done.1 = f32[2,4,256,256]{3,2,1,0:T(8,128)S(1)} collective-permute-done((f32[2,4,256,256]{3,2,1,0:T(8,128)S(1)}, f32[2,4,256,256]{3,2,1,0:T(8,128)S(1)}, u32[]{:S(2)}, u32[]{:S(2)}) %collective-permute-start.1) | collective-permute-done | bytes 2097184 | tf_op jit(solution)/shard_map/ppermute | solution.py:13
  59.6 2.5 collective-permute-start.2
  62.0 0.5 collective-permute-done.4
  62.5 1.3 copy-done.4
  63.9 1.2 collective-permute-start.5
  65.1 19.9 %collective-permute-done.2 = f32[2,4,256,256]{3,2,1,0:T(8,128)} collective-permute-done((f32[2,4,256,256]{3,2,1,0:T(8,128)S(1)}, f32[2,4,256,256]{3,2,1,0:T(8,128)}, u32[]{:S(2)}, u32[]{:S(2)}) %collective-permute-start.2) | collective-permute-done | bytes 2097184 | tf_op jit(solution)/shard_map/ppermute | solution.py:13
  85.0 2.6 collective-permute-start.3
  87.6 2.1 collective-permute-done.5
  89.7 1.8 collective-permute-start.6
  91.6 0.7 slice_reduce_fusion
  92.6 18.3 %collective-permute-done.3 = f32[2,4,256,256]{3,2,1,0:T(8,128)} collective-permute-done((f32[2,4,256,256]{3,2,1,0:T(8,128)}, f32[2,4,256,256]{3,2,1,0:T(8,128)}, u32[]{:S(2)}, u32[]{:S(2)}) %collective-permute-start.3) | collective-permute-done | bytes 2097184 | tf_op jit(solution)/shard_map/ppermute | solution.py:13
  110.9 1.8 constant_dynamic-update-slice_fusion.15
  112.7 1.8 constant_dynamic-update-slice_fusion.14
  114.5 2.0 constant_dynamic-update-slice_fusion.13
  116.5 2.0 constant_dynamic-update-slice_fusion.12
  118.8 1.8 constant_dynamic-update-slice_fusion.9
  120.7 1.8 constant_dynamic-update-slice_fusion.8
  122.5 1.8 constant_dynamic-update-slice_fusion.7
  124.3 1.8 constant_dynamic-update-slice_fusion.6
  126.8 1.8 constant_dynamic-update-slice_fusion.1
  128.6 1.8 constant_dynamic-update-slice_fusion
  130.5 6.3 %constant_dynamic-slice_fusion.3 = f32[2,32,256,256]{3,2,1,0:T(8,128)} fusion(f32[2,64,256,256]{3,2,1,0:T(8,128)S(1)} %constant_dynamic-update-slice_fusion, s32[]{:T(128)S(6)} %select_n.81), kind=kLoop, calls=%fused_computation.71 | loop fusion | bytes 33554436 | tf_op jit(solution)/shard_map/jit(_roll_dynamic)/dynamic_slice | solution.py:17
  136.8 7.8 %broadcast_in_dim.2 = f32[64,256,256]{2,1,0:T(8,128)} broadcast(f32[]{:T(128)} %constant.89.clone.1), dimensions={} | broadcast | bytes 16777220 | tf_op jit(solution)/shard_map/broadcast_in_dim | solution.py:60
  144.6 74.3 %while.10 = (s32[]{:T(128)}, f32[64,256,256]{2,1,0:T(8,128)}, s32[4,8]{1,0:T(4,128)S(1)}, s32[4,8]{1,0:T(4,128)S(1)}, f32[4,256,256]{2,1,0:T(8,128)S(1)}, /*inde...) while((s32[]{:T(128)}, f32[64,256,256]{2,1,0:T(8,128)}, s32[4,8]{1,0:T(4,128)S(1)}, ...), condition=%wide.region_2.3_spmd, body=%wide.region_0.2_spmd.sunk | while | flops 1611139200 | bytes 20980156 | solution.py:62
  144.6 2.0 gather_fusion
  146.7 7.8 %gather_fusion.1 = f32[8,256,256]{2,1,0:T(8,128)} fusion(f32[64,256,256]{2,1,0:T(8,128)} %get-tuple-element.133, s32[1024]{0:T(1024)S(1)} %pad_clamp_fusion.5), kind=kCustom, calls=%fused_computation.1.clone.1 | custom fusion | bytes 4194336 | tf_op jit(solution)/shard_map/while/body/eval_jaxpr/gather | solution.py:54
  154.5 4.3 fusion.34
  158.8 4.4 scatter_fusion
  163.2 2.0 gather_fusion
  165.2 7.8 %gather_fusion.1 = f32[8,256,256]{2,1,0:T(8,128)} fusion(f32[64,256,256]{2,1,0:T(8,128)} %get-tuple-element.133, s32[1024]{0:T(1024)S(1)} %pad_clamp_fusion.5), kind=kCustom, calls=%fused_computation.1.clone.1 | custom fusion | bytes 4194336 | tf_op jit(solution)/shard_map/while/body/eval_jaxpr/gather | solution.py:54
  173.1 4.3 fusion.34
  177.4 4.4 scatter_fusion
  181.8 2.0 gather_fusion
  183.8 7.8 %gather_fusion.1 = f32[8,256,256]{2,1,0:T(8,128)} fusion(f32[64,256,256]{2,1,0:T(8,128)} %get-tuple-element.133, s32[1024]{0:T(1024)S(1)} %pad_clamp_fusion.5), kind=kCustom, calls=%fused_computation.1.clone.1 | custom fusion | bytes 4194336 | tf_op jit(solution)/shard_map/while/body/eval_jaxpr/gather | solution.py:54
  191.7 4.3 fusion.34
  196.0 4.4 scatter_fusion
  200.4 2.0 gather_fusion
  202.4 7.8 %gather_fusion.1 = f32[8,256,256]{2,1,0:T(8,128)} fusion(f32[64,256,256]{2,1,0:T(8,128)} %get-tuple-element.133, s32[1024]{0:T(1024)S(1)} %pad_clamp_fusion.5), kind=kCustom, calls=%fused_computation.1.clone.1 | custom fusion | bytes 4194336 | tf_op jit(solution)/shard_map/while/body/eval_jaxpr/gather | solution.py:54
  210.2 4.3 fusion.34
  214.6 4.4 scatter_fusion
  219.0 0.6 copy-done.9
  219.6 0.6 dynamic-slice
  220.8 223.1 %all-reduce.3.cloned.1.call-done = f32[2,32,256,256]{3,2,1,0:T(8,128)} async-done(((f32[2,32,256,256]{3,2,1,0:T(8,128)}), f32[2,32,256,256]{3,2,1,0:T(8,128)}) %all-reduce.3.cloned.1.call-update) | async-done | bytes 16777232
  444.0 2.3 dynamic-slice_add_fusion
  (48 shorter events, 1.7 us)
Async XLA Ops:
  6.5 112.0 %copy-start.1 = (f32[2,4,256,256]{3,2,1,0:T(8,128)S(1)}, f32[2,4,256,256]{3,2,1,0:T(8,128)}, u32[]{:S(2)}) copy-start(f32[2,4,256,256]{3,2,1,0:T(8,128)} %param.7) | copy-start | bytes 6291460
  6.5 437.4 %all-reduce.3.cloned.1.call-start = ((), (), s32[]{:S(2)}) async-start(), calls=%async_computation | async-start | bytes 33554432
  6.5 26.3 %collective-permute-start = (f32[2,4,256,256]{3,2,1,0:T(8,128)}, f32[2,4,256,256]{3,2,1,0:T(8,128)S(1)}, u32[]{:S(2)}, u32[]{:S(2)}) collective-permute-start(f32[2,4,256,256]{3,2,1,0:T(8,128)} %param.7), channel_id=1, source_target_pairs={{0,16},{16,32},{32,48},{48,64},{64,80},{80,96},{96,112},{112,0},{1... | collective-permute-start | bytes 6291464 | tf_op jit(solution)/shard_map/ppermute | solution.py:13
  32.9 1.3 copy-start.2
  34.2 25.4 %collective-permute-start.1 = (f32[2,4,256,256]{3,2,1,0:T(8,128)S(1)}, f32[2,4,256,256]{3,2,1,0:T(8,128)S(1)}, u32[]{:S(2)}, u32[]{:S(2)}) collective-permute-start(f32[2,4,256,256]{3,2,1,0:T(8,128)S(1)} %collective-permute-done), channel_id=1, source_target_pairs={{0,16},{16,32},{32,48},{48,64},{64,80},{80,96},{96,112},{112,0},{1... | collective-permute-start | bytes 6291464 | tf_op jit(solution)/shard_map/ppermute | solution.py:13
  36.6 26.0 %collective-permute-start.4 = (f32[2,4,256,256]{3,2,1,0:T(8,128)}, f32[2,4,256,256]{3,2,1,0:T(8,128)S(1)}, u32[]{:S(2)}, u32[]{:S(2)}) collective-permute-start(f32[2,4,256,256]{3,2,1,0:T(8,128)} %param.7), channel_id=1, source_target_pairs={{0,112},{16,0},{32,16},{48,32},{64,48},{80,64},{96,80},{112,96},{1... | collective-permute-start | bytes 6291464 | tf_op jit(solution)/shard_map/ppermute | solution.py:15
  59.6 30.2 %copy-start.6 = (f32[2,4,256,256]{3,2,1,0:T(8,128)}, f32[2,4,256,256]{3,2,1,0:T(8,128)S(1)}, u32[]{:S(2)}) copy-start(f32[2,4,256,256]{3,2,1,0:T(8,128)S(1)} %collective-permute-done.1) | copy-start | bytes 6291460
  59.6 25.5 %collective-permute-start.2 = (f32[2,4,256,256]{3,2,1,0:T(8,128)S(1)}, f32[2,4,256,256]{3,2,1,0:T(8,128)}, u32[]{:S(2)}, u32[]{:S(2)}) collective-permute-start(f32[2,4,256,256]{3,2,1,0:T(8,128)S(1)} %collective-permute-done.1), channel_id=1, source_target_pairs={{0,16},{16,32},{32,48},{48,64},{64,80},{80,96},{96,112},{112,0},{1... | collective-permute-start | bytes 6291464 | tf_op jit(solution)/shard_map/ppermute | solution.py:13
  62.5 1.3 copy-start.4
  63.9 25.9 %collective-permute-start.5 = (f32[2,4,256,256]{3,2,1,0:T(8,128)S(1)}, f32[2,4,256,256]{3,2,1,0:T(8,128)}, u32[]{:S(2)}, u32[]{:S(2)}) collective-permute-start(f32[2,4,256,256]{3,2,1,0:T(8,128)S(1)} %collective-permute-done.4), channel_id=1, source_target_pairs={{0,112},{16,0},{32,16},{48,32},{64,48},{80,64},{96,80},{112,96},{1... | collective-permute-start | bytes 6291464 | tf_op jit(solution)/shard_map/ppermute | solution.py:15
  85.0 25.9 %collective-permute-start.3 = (f32[2,4,256,256]{3,2,1,0:T(8,128)}, f32[2,4,256,256]{3,2,1,0:T(8,128)}, u32[]{:S(2)}, u32[]{:S(2)}) collective-permute-start(f32[2,4,256,256]{3,2,1,0:T(8,128)} %collective-permute-done.2), channel_id=1, source_target_pairs={{0,16},{16,32},{32,48},{48,64},{64,80},{80,96},{96,112},{112,0},{1... | collective-permute-start | bytes 6291464 | tf_op jit(solution)/shard_map/ppermute | solution.py:13
  89.7 30.9 %collective-permute-start.6 = (f32[2,4,256,256]{3,2,1,0:T(8,128)}, f32[2,4,256,256]{3,2,1,0:T(8,128)}, u32[]{:S(2)}, u32[]{:S(2)}) collective-permute-start(f32[2,4,256,256]{3,2,1,0:T(8,128)} %collective-permute-done.5), channel_id=1, source_target_pairs={{0,112},{16,0},{32,16},{48,32},{64,48},{80,64},{96,80},{112,96},{1... | collective-permute-start | bytes 6291464 | tf_op jit(solution)/shard_map/ppermute | solution.py:15
  92.5 26.1 %copy-start.5 = (f32[2,4,256,256]{3,2,1,0:T(8,128)S(1)}, f32[2,4,256,256]{3,2,1,0:T(8,128)}, u32[]{:S(2)}) copy-start(f32[2,4,256,256]{3,2,1,0:T(8,128)} %copy-done.4) | copy-start | bytes 6291460
  114.5 11.6 %copy-start.7 = (f32[2,4,256,256]{3,2,1,0:T(8,128)S(1)}, f32[2,4,256,256]{3,2,1,0:T(8,128)}, u32[]{:S(2)}) copy-start(f32[2,4,256,256]{3,2,1,0:T(8,128)} %copy-done.6) | copy-start | bytes 6291460
  116.5 9.8 %copy-start.3 = (f32[2,4,256,256]{3,2,1,0:T(8,128)S(1)}, f32[2,4,256,256]{3,2,1,0:T(8,128)}, u32[]{:S(2)}) copy-start(f32[2,4,256,256]{3,2,1,0:T(8,128)} %copy-done.2) | copy-start | bytes 6291460
  136.8 7.8 %copy-start = (f32[2,2,256,256]{3,2,1,0:T(8,128)S(1)}, f32[2,2,256,256]{3,2,1,0:T(8,128)}, u32[]{:S(2)}) copy-start(f32[2,2,256,256]{3,2,1,0:T(8,128)} %param.6) | copy-start | bytes 3145732
  219.0 0.7 copy-start.9
  219.0 225.0 %copy-start.8 = (f32[2,2,256,256]{3,2,1,0:T(8,128)S(1)}, f32[2,2,256,256]{3,2,1,0:T(8,128)}, u32[]{:S(2)}) copy-start(f32[2,2,256,256]{3,2,1,0:T(8,128)} %param.8) | copy-start | bytes 3145732
Sparse Core Ops, SparseCore 0:
  219.1 224.8 all-reduce.2
